TPU v7x, 512 devices: a whole 4x8x8 slice. The times are simulated.
512 devices in a mesh: slab: 32 (over y, x), sub: 16 (over z, core).
Axes of the slice: x: 4, y: 8, z: 8, core: 2. Of those that a mesh axis runs over, the one named last changes fastest.
Arguments:
- positions: float32 [3, 524288], P(None, 'slab'), may hold values from 0 to 129, as said below
- velocity: float32 [3, 524288], P(None, 'slab'), may hold values from -6 to 6
- density: float32 [524288], P('slab'), may hold values from 0.1 to 10
- pressure: float32 [524288], P('slab'), may hold values from 0.1 to 10
- counts: int32 [4096], P('slab'), may hold values from 8 to 128, as said below
- pair_list: int32 [3, 20480], P(None, ('slab', 'sub')), may hold values from -128 to 4095, as said below
Outputs:
- rates: float32 [5, 524288], P(None, 'slab')
Inputs may be any that keep to these rules, and one draw needn't show every extreme that they name: `positions`: particle k of leaf g lies in slab floor(g / 128) along x (x minus that index in [0, 1)), in column g mod 128 along y (likewise), and z in [0, 1). `counts`: at least 8 live particles a leaf; some leaf holds 128. `pair_list`: row 0 is a slot's home leaf, a leaf of this device's part of its slab (columns 8 * i to 8 * i + 7 on the device of index i along sub), or -1 for an empty slot. Row 1 is the other leaf, -1 for an empty slot: the home leaf itself, the leaf of the next column cyclically in the same slab, or a leaf of the next slab cyclically whose column is the home column - 1, + 0 or + 1 plus w, modulo 128; w is 0 for home leaves outside the last slab and one shift common to all pairs headed in the last slab. Row 2 is the image offset along y in units of cell width, 0 for an empty slot and for a pair of a leaf with itself; for a pair into the next slab, minus row 2 modulo 128 equals w. A leaf heads at most 5 pairs, each device holds at most 40 live slots, and some device holds exactly that many.
All inputs are finite; a program needn't handle non-finite values.
Results may differ from a plain program's by a relative error of at most 0.0003.
Values sent between devices are 32-bit elements; how exact they have to be, the bound alone decides.
A program may use at most 64 MiB of HBM per device.

v0:
```python
import math
import jax
import jax.numpy as jnp
from jax import lax
from jax.sharding import PartitionSpec as P

LEAF = 128
CAND = 5
GAMMA = 5.0 / 3.0
SUPPORT = 1.5
KERNEL_NORM = 21.0 / (2.0 * math.pi * SUPPORT**3)
MOMENT_REG = 0.05
SHEAR_SPEED = 1.0
AREA_FLOOR = 0.0001
SYM_PAIRS = ((0, 0), (0, 1), (0, 2), (1, 1), (1, 2), (2, 2))
UNIT_DIAG = (1.0, 0.0, 0.0, 1.0, 0.0, 1.0)


def shifted(shard, axis, by):
    peers = lax.axis_size(axis)
    return lax.ppermute(shard, axis, [(i, (i + by) % peers) for i in range(peers)])


def kernel(dist_sq):
    scaled = jnp.sqrt(dist_sq) / SUPPORT
    inside = jnp.maximum(1.0 - scaled, 0.0)
    return KERNEL_NORM * inside**4 * (1.0 + 4.0 * scaled)


def image_rows(tile, wrapped, offset, box_length):
    zero_row = jnp.zeros_like(offset)
    displace = jnp.stack(
        [
            wrapped * box_length,
            offset,
            zero_row,
            zero_row,
            -SHEAR_SPEED * wrapped,
            zero_row,
            zero_row,
            zero_row,
        ]
    )
    return tile + displace[:, :, None]


def sym_apply(matrix, vector):
    comp_x = matrix[0] * vector[0] + matrix[1] * vector[1] + matrix[2] * vector[2]
    comp_y = matrix[1] * vector[0] + matrix[3] * vector[1] + matrix[4] * vector[2]
    comp_z = matrix[2] * vector[0] + matrix[4] * vector[1] + matrix[5] * vector[2]
    return [comp_x, comp_y, comp_z]


def sym_inverse(matrix):
    entry_xx, entry_xy, entry_xz, entry_yy, entry_yz, entry_zz = matrix
    minor_xx = entry_yy * entry_zz - entry_yz * entry_yz
    minor_xy = entry_xz * entry_yz - entry_xy * entry_zz
    minor_xz = entry_xy * entry_yz - entry_xz * entry_yy
    minor_yy = entry_xx * entry_zz - entry_xz * entry_xz
    minor_yz = entry_xy * entry_xz - entry_xx * entry_yz
    minor_zz = entry_xx * entry_yy - entry_xy * entry_xy
    determinant = entry_xx * minor_xx + entry_xy * minor_xy + entry_xz * minor_xz
    return [
        minor / determinant
        for minor in (minor_xx, minor_xy, minor_xz, minor_yy, minor_yz, minor_zz)
    ]


def moment_tile(near_tile, far_tile, mask_near, mask_far, weight):
    separation = [
        far_tile[direction][:, None, :] - near_tile[direction][:, :, None] for direction in range(3)
    ]
    dist_sq = (
        separation[0] * separation[0]
        + separation[1] * separation[1]
        + separation[2] * separation[2]
    )
    smoothing = (
        kernel(dist_sq) * mask_near[:, :, None] * mask_far[:, None, :] * weight[:, None, None]
    )
    summands = [smoothing] + [
        smoothing * separation[left_axis] * separation[right_axis]
        for left_axis, right_axis in SYM_PAIRS
    ]
    for quantity in range(5):
        weighted = smoothing * (
            far_tile[3 + quantity][:, None, :] - near_tile[3 + quantity][:, :, None]
        )
        summands = summands + [weighted * separation[direction] for direction in range(3)]
    row_sums = jnp.stack([jnp.sum(summand, axis=2) for summand in summands])
    col_sums = jnp.stack([jnp.sum(summand, axis=1) for summand in summands])
    return (row_sums, col_sums)


def finish_moments(moments, live_mask):
    number_density = moments[0] + 1.0 - live_mask
    inverse_density = 1.0 / number_density
    second = [
        moments[1 + position] * inverse_density + MOMENT_REG * UNIT_DIAG[position]
        for position in range(6)
    ]
    inverse = sym_inverse(second)
    slopes = []
    for quantity in range(5):
        numerator = [
            moments[7 + 3 * quantity + direction] * inverse_density for direction in range(3)
        ]
        slopes = slopes + sym_apply(inverse, numerator)
    return jnp.stack([number_density] + inverse + slopes)


def side_flux(
    density_side, velocity_side, pressure_side, normal, normal_speed, lag_speed, wave_speed, contact
):
    energy = pressure_side / (GAMMA - 1.0) + 0.5 * density_side * (
        velocity_side[0] ** 2 + velocity_side[1] ** 2 + velocity_side[2] ** 2
    )
    plain_flux = [density_side * normal_speed]
    plain_flux = plain_flux + [
        density_side * velocity_side[direction] * normal_speed + pressure_side * normal[direction]
        for direction in range(3)
    ]
    plain_flux = plain_flux + [(energy + pressure_side) * normal_speed]
    conserved = (
        [density_side]
        + [density_side * velocity_side[direction] for direction in range(3)]
        + [energy]
    )
    factor = density_side * lag_speed / (wave_speed - contact)
    speed_gap = contact - normal_speed
    star_state = [factor] + [
        factor * (velocity_side[direction] + speed_gap * normal[direction])
        for direction in range(3)
    ]
    star_state = star_state + [
        factor
        * (
            energy / density_side
            + speed_gap * (contact + pressure_side / (density_side * lag_speed))
        )
    ]
    starred = [
        plain_flux[component] + wave_speed * (star_state[component] - conserved[component])
        for component in range(5)
    ]
    return (plain_flux, starred)


def hllc_flux(left_state, right_state, normal, face_vel):
    left_vel = [left_state[direction] - face_vel[direction] for direction in range(3)]
    right_vel = [right_state[direction] - face_vel[direction] for direction in range(3)]
    left_density, left_pressure = (left_state[3], left_state[4])
    right_density, right_pressure = (right_state[3], right_state[4])
    left_normal = left_vel[0] * normal[0] + left_vel[1] * normal[1] + left_vel[2] * normal[2]
    right_normal = right_vel[0] * normal[0] + right_vel[1] * normal[1] + right_vel[2] * normal[2]
    left_sound = jnp.sqrt(GAMMA * left_pressure / left_density)
    right_sound = jnp.sqrt(GAMMA * right_pressure / right_density)
    speed_left = jnp.minimum(left_normal - left_sound, right_normal - right_sound)
    speed_right = jnp.maximum(left_normal + left_sound, right_normal + right_sound)
    lag_left = speed_left - left_normal
    lag_right = speed_right - right_normal
    contact = (
        right_pressure
        - left_pressure
        + left_density * left_normal * lag_left
        - right_density * right_normal * lag_right
    ) / (left_density * lag_left - right_density * lag_right)
    flux_left, star_left = side_flux(
        left_density, left_vel, left_pressure, normal, left_normal, lag_left, speed_left, contact
    )
    flux_right, star_right = side_flux(
        right_density,
        right_vel,
        right_pressure,
        normal,
        right_normal,
        lag_right,
        speed_right,
        contact,
    )
    moving = [
        jnp.where(
            speed_left >= 0.0,
            flux_left[component],
            jnp.where(
                contact >= 0.0,
                star_left[component],
                jnp.where(speed_right >= 0.0, star_right[component], flux_right[component]),
            ),
        )
        for component in range(5)
    ]
    mass_flux = moving[0]
    momentum = [moving[1 + direction] + face_vel[direction] * mass_flux for direction in range(3)]
    face_sq = face_vel[0] ** 2 + face_vel[1] ** 2 + face_vel[2] ** 2
    energy_flux = (
        moving[4]
        + face_vel[0] * moving[1]
        + face_vel[1] * moving[2]
        + face_vel[2] * moving[3]
        + 0.5 * face_sq * mass_flux
    )
    return [mass_flux] + momentum + [energy_flux]


def flux_tile(near_tile, far_tile, near_pay, far_pay, mask_near, mask_far, weight):
    separation = [
        far_tile[direction][:, None, :] - near_tile[direction][:, :, None] for direction in range(3)
    ]
    dist_sq = (
        separation[0] * separation[0]
        + separation[1] * separation[1]
        + separation[2] * separation[2]
    )
    smoothing = kernel(dist_sq) * mask_near[:, :, None] * mask_far[:, None, :]
    near_density = near_pay[0][:, :, None]
    far_density = far_pay[0][:, None, :]
    near_matrix = [near_pay[1 + position][:, :, None] for position in range(6)]
    far_matrix = [far_pay[1 + position][:, None, :] for position in range(6)]
    toward_near = sym_apply(near_matrix, separation)
    toward_far = sym_apply(far_matrix, separation)
    near_scale = smoothing / (near_density * near_density)
    far_scale = smoothing / (far_density * far_density)
    area = [
        near_scale * toward_near[direction] + far_scale * toward_far[direction]
        for direction in range(3)
    ]
    magnitude = jnp.sqrt(area[0] * area[0] + area[1] * area[1] + area[2] * area[2])
    clamp_scale = 1.0 / jnp.maximum(magnitude, AREA_FLOOR)
    normal = [area[direction] * clamp_scale for direction in range(3)]
    left_state = []
    right_state = []
    for quantity in range(5):
        near_value = near_tile[3 + quantity][:, :, None]
        far_value = far_tile[3 + quantity][:, None, :]
        near_change = 0.5 * (
            near_pay[7 + 3 * quantity][:, :, None] * separation[0]
            + near_pay[8 + 3 * quantity][:, :, None] * separation[1]
            + near_pay[9 + 3 * quantity][:, :, None] * separation[2]
        )
        far_change = 0.5 * (
            far_pay[7 + 3 * quantity][:, None, :] * separation[0]
            + far_pay[8 + 3 * quantity][:, None, :] * separation[1]
            + far_pay[9 + 3 * quantity][:, None, :] * separation[2]
        )
        low_bound = jnp.minimum(near_value, far_value)
        high_bound = jnp.maximum(near_value, far_value)
        left_state.append(jnp.clip(near_value + near_change, low_bound, high_bound))
        right_state.append(jnp.clip(far_value - far_change, low_bound, high_bound))
    face_vel = [
        0.5 * (near_tile[3 + direction][:, :, None] + far_tile[3 + direction][:, None, :])
        for direction in range(3)
    ]
    fluxes = hllc_flux(left_state, right_state, normal, face_vel)
    pair_scale = magnitude * weight[:, None, None]
    row_sums = jnp.stack([-jnp.sum(pair_scale * face_flux, axis=2) for face_flux in fluxes])
    col_sums = jnp.stack([jnp.sum(pair_scale * face_flux, axis=1) for face_flux in fluxes])
    return (row_sums, col_sums)


def shards(positions, velocity, density, pressure, counts, pair_list):
    slab_leaves = counts.shape[0]
    slab_count = lax.axis_size("slab")
    slab_index = lax.axis_index("slab")
    state = jnp.concatenate([positions, velocity, density[None], pressure[None]], axis=0)
    upper_state, upper_counts = shifted((state, counts.astype(jnp.float32)), "slab", -1)
    slab_state = state.reshape(8, slab_leaves, LEAF)
    upper_slab = upper_state.reshape(8, slab_leaves, LEAF)
    upper_whole = upper_counts.astype(jnp.int32)
    box_length = jnp.asarray(slab_count, jnp.float32)
    slot_count = pair_list.shape[1]
    ranking = jnp.argsort((pair_list[0] < 0).astype(jnp.int32), stable=True)
    slots = pair_list[:, ranking]
    live_count = jnp.sum((pair_list[0] >= 0).astype(jnp.int32))
    occupied = slots[0] >= 0
    home_leaf = jnp.where(occupied, slots[0], 0)
    other_leaf = jnp.where(occupied, slots[1], 0)
    wrapped = (other_leaf // slab_leaves < home_leaf // slab_leaves).astype(jnp.float32)
    offset = slots[2].astype(jnp.float32)
    weight = jnp.where(occupied, jnp.where(home_leaf == other_leaf, 0.5, 1.0), 0.0).astype(
        jnp.float32
    )
    base_leaf = slab_index * slab_leaves
    turns = (live_count + CAND - 1) // CAND
    window = jnp.concatenate([slab_state, upper_slab], axis=1)
    window_counts = jnp.concatenate([counts, upper_whole])
    width = 2 * slab_leaves
    home_window = jnp.where(occupied, home_leaf - base_leaf, 0)
    other_window = jnp.where(occupied, (other_leaf - base_leaf) % (slab_count * slab_leaves), 0)
    window_mask = (jnp.arange(LEAF, dtype=jnp.int32)[None, :] < window_counts[:, None]).astype(
        jnp.float32
    )
    leaf_ids = jnp.arange(width, dtype=jnp.int32)
    home_hot = (home_window[:, None] == leaf_ids[None, :]).astype(jnp.float32)
    other_hot = (other_window[:, None] == leaf_ids[None, :]).astype(jnp.float32)

    def sweep(tile_fn, row_count):

        def one_turn(turn_index, buffers):
            row_buffer, col_buffer = buffers
            first_slot = turn_index * CAND
            home_part = lax.dynamic_slice_in_dim(home_window, first_slot, CAND)
            other_part = lax.dynamic_slice_in_dim(other_window, first_slot, CAND)
            wrap_part = lax.dynamic_slice_in_dim(wrapped, first_slot, CAND)
            offset_part = lax.dynamic_slice_in_dim(offset, first_slot, CAND)
            weight_part = lax.dynamic_slice_in_dim(weight, first_slot, CAND)
            row_sums, col_sums = tile_fn(home_part, other_part, wrap_part, offset_part, weight_part)
            row_buffer = lax.dynamic_update_slice_in_dim(row_buffer, row_sums, first_slot, 1)
            col_buffer = lax.dynamic_update_slice_in_dim(col_buffer, col_sums, first_slot, 1)
            return (row_buffer, col_buffer)

        empty = jnp.zeros((row_count, slot_count, LEAF), jnp.float32)
        row_buffer, col_buffer = lax.fori_loop(0, turns, one_turn, (empty, empty))
        total = jnp.einsum("rsp,sw->rwp", row_buffer, home_hot, precision=lax.Precision.HIGHEST)
        return total + jnp.einsum(
            "rsp,sw->rwp", col_buffer, other_hot, precision=lax.Precision.HIGHEST
        )

    def settle(partial_value):
        row_count = partial_value.shape[0]
        partial_value = lax.psum(partial_value, "sub")
        own_part = partial_value[:, :slab_leaves]
        next_part = partial_value[:, slab_leaves:]
        returned = shifted(next_part, "slab", 1)
        merged = own_part + returned
        return merged

    def moment_fn(home_part, other_part, wrap_part, offset_part, weight_part):
        near_tile = jnp.take(window, home_part, axis=1)
        far_tile = image_rows(
            jnp.take(window, other_part, axis=1), wrap_part, offset_part, box_length
        )
        return moment_tile(
            near_tile, far_tile, window_mask[home_part], window_mask[other_part], weight_part
        )

    moments = settle(sweep(moment_fn, 22))
    own_count = moments.shape[1]
    payload = finish_moments(moments, window_mask[:own_count])
    arrived = shifted(payload, "slab", -1)
    window_payload = jnp.concatenate([payload, arrived], axis=1)

    def flux_fn(home_part, other_part, wrap_part, offset_part, weight_part):
        near_tile = jnp.take(window, home_part, axis=1)
        far_tile = image_rows(
            jnp.take(window, other_part, axis=1), wrap_part, offset_part, box_length
        )
        near_pay = jnp.take(window_payload, home_part, axis=1)
        far_pay = jnp.take(window_payload, other_part, axis=1)
        return flux_tile(
            near_tile,
            far_tile,
            near_pay,
            far_pay,
            window_mask[home_part],
            window_mask[other_part],
            weight_part,
        )

    flux_sum = settle(sweep(flux_fn, 5))
    rate_part = (payload[0][None] * flux_sum).reshape(5, own_count * LEAF)
    return rate_part


def solution(mesh):
    placed = (
        P(None, "slab"),
        P(None, "slab"),
        P("slab"),
        P("slab"),
        P("slab"),
        P(None, ("slab", "sub")),
    )
    return jax.shard_map(
        shards, mesh=mesh, in_specs=placed, out_specs=P(None, "slab"), check_vma=False
    )
```

profile of v0, /device:TPU:1, one launch (start us, length us, event | category | flops | bytes accessed | tf_op | source)
XLA Modules:
  0.0 1030.1 jit_solution(6164458053880758125)
XLA Ops:
  7.3 8.1 collective-permute-start.1
  16.7 2.5 collective-permute-start
  22.6 2.0 sort.17
  28.0 3.1 collective-permute-done
  32.4 74.5 %while.30 = (s32[]{:T(128)}, f32[22,40,128]{2,1,0:T(8,128)S(1)}, f32[22,40,128]{2,1,0:T(8,128)S(1)}, s32[]{:T(128)}, s32[40]{0:T(128)}, /*index=5*/f32[8,256,128...) while((s32[]{:T(128)}, f32[22,40,128]{2,1,0:T(8,128)S(1)}, ...), condition=%wide.region_47.49_spmd.clone, body=%wide.region_2.48_spmd.clone.sunk | while | flops 9721420 | bytes 1241347 | solution.py:313
  37.0 2.9 fusion.246
  46.4 2.9 fusion.246
  55.7 2.9 fusion.246
  65.0 2.9 fusion.246
  74.3 2.9 fusion.246
  83.6 2.9 fusion.246
  92.9 2.9 fusion.246
  102.3 2.9 fusion.246
  108.9 3.9 add_bitcast_fusion
  112.9 126.5 %all-reduce.3.cloned.1.call-done = f32[22,256,128]{2,1,0:T(8,128)} async-done(((f32[22,256,128]{2,1,0:T(8,128)}), f32[22,256,128]{2,1,0:T(8,128)}) %all-reduce.3.cloned.1.call-update) | async-done | bytes 2883600 | tf_op jit(solution)/shard_map/psum | solution.py:321
  240.9 3.1 collective-permute-start.2
  244.1 34.1 %collective-permute-done.2 = f32[22,128,128]{2,1,0:T(8,128)S(1)} collective-permute-done((f32[22,128,128]{2,1,0:T(8,128)S(1)}, f32[22,128,128]{2,1,0:T(8,128)S(1)}, u32[]{:S(2)}, u32[]{:S(2)}) %collective-permute-start.2) | collective-permute-done | bytes 1441824 | tf_op jit(solution)/shard_map/ppermute | solution.py:21
  279.4 3.4 collective-permute-start.3
  282.8 29.6 %collective-permute-done.3 = f32[22,128,128]{2,1,0:T(8,128)S(1)} collective-permute-done((f32[22,128,128]{2,1,0:T(8,128)S(1)}, f32[22,128,128]{2,1,0:T(8,128)S(1)}, u32[]{:S(2)}, u32[]{:S(2)}) %collective-permute-start.3) | collective-permute-done | bytes 1441824 | tf_op jit(solution)/shard_map/ppermute | solution.py:21
  315.0 570.6 %while.31 = (s32[]{:T(128)}, f32[5,40,128]{2,1,0:T(8,128)}, f32[5,40,128]{2,1,0:T(8,128)S(1)}, s32[]{:T(128)}, s32[40]{0:T(128)}, /*index=5*/f32[8,256,128]{2,0,...) while((s32[]{:T(128)}, f32[5,40,128]{2,1,0:T(8,128)}, ...), condition=%wide.region_60.63_spmd.clone, body=%wide.region_49.62_spmd.clone.sunk | while | flops 113486544 | bytes 2761233 | solution.py:313
  353.4 6.3 fusion.254
  359.8 5.9 fusion.253
  365.7 6.3 fusion.255
  372.3 5.6 fusion.256
  377.9 6.8 fusion.257
  424.7 6.3 fusion.254
  431.1 5.9 fusion.253
  437.0 6.3 fusion.255
  443.6 5.6 fusion.256
  449.3 6.8 fusion.257
  496.0 6.3 fusion.254
  502.4 5.9 fusion.253
  508.3 6.3 fusion.255
  514.9 5.6 fusion.256
  520.6 6.8 fusion.257
  567.3 6.3 fusion.254
  573.7 5.9 fusion.253
  579.7 6.3 fusion.255
  586.2 5.6 fusion.256
  591.9 6.8 fusion.257
  638.7 6.3 fusion.254
  645.0 5.9 fusion.253
  651.0 6.3 fusion.255
  657.6 5.6 fusion.256
  663.2 6.8 fusion.257
  710.0 6.3 fusion.254
  716.4 5.9 fusion.253
  722.3 6.3 fusion.255
  728.9 5.6 fusion.256
  734.5 6.8 fusion.257
  781.3 6.3 fusion.254
  787.7 5.9 fusion.253
  793.6 6.3 fusion.255
  800.2 5.6 fusion.256
  805.9 6.8 fusion.257
  852.6 6.3 fusion.254
  859.0 5.9 fusion.253
  864.9 6.3 fusion.255
  871.5 5.6 fusion.256
  877.2 6.8 fusion.257
  887.0 2.1 fusion.153
  889.1 117.4 %all-reduce.5.cloned.1.call-done = f32[5,256,128]{2,1,0:T(8,128)} async-done(((f32[5,256,128]{2,1,0:T(8,128)}), f32[5,256,128]{2,1,0:T(8,128)}) %all-reduce.5.cloned.1.call-update) | async-done | bytes 655376 | tf_op jit(solution)/shard_map/psum | solution.py:321
  1007.5 3.1 collective-permute-start.4
  1010.6 10.7 %collective-permute-done.4 = f32[5,128,128]{2,1,0:T(8,128)S(1)} collective-permute-done((f32[5,128,128]{2,1,0:T(8,128)S(1)}, f32[5,128,128]{2,1,0:T(8,128)S(1)}, u32[]{:S(2)}, u32[]{:S(2)}) %collective-permute-start.4) | collective-permute-done | bytes 327712 | tf_op jit(solution)/shard_map/ppermute | solution.py:21
  (2204 shorter events, 384.3 us)
Async XLA Ops:
  6.5 232.8 %all-reduce.3.cloned.1.call-start = ((), (), s32[]{:S(2)}) async-start(), calls=%async_computation | async-start | bytes 5767168 | tf_op jit(solution)/shard_map/psum | solution.py:321
  7.3 20.1 %collective-permute-start.1 = (f32[128]{0:T(128)S(1)}, f32[128]{0:T(128)S(1)}, u32[]{:S(2)}, u32[]{:S(2)}) collective-permute-start(f32[128]{0:T(128)S(1)} %convert_element_type.36), channel_id=1, source_target_pairs={{0,496},{16,0},{32,16},{48,32},{64,48},{80,64},{96,80},{112,96},{1... | collective-permute-start | bytes 1544 | tf_op jit(solution)/shard_map/ppermute | solution.py:21
  16.7 14.4 %collective-permute-start = (f32[8,16384]{1,0:T(8,128)S(1)}, f32[8,16384]{1,0:T(8,128)S(1)}, u32[]{:S(2)}, u32[]{:S(2)}) collective-permute-start(f32[8,16384]{1,0:T(8,128)S(1)} %pad_maximum_fusion.2), channel_id=1, source_target_pairs={{0,496},{16,0},{32,16},{48,32},{64,48},{80,64},{96,80},{112,96},{1... | collective-permute-start | bytes 1572872 | tf_op jit(solution)/shard_map/ppermute | solution.py:21
  112.8 893.7 %all-reduce.5.cloned.1.call-start = ((), (), s32[]{:S(2)}) async-start(), calls=%async_computation.1 | async-start | bytes 1310720 | tf_op jit(solution)/shard_map/psum | solution.py:321
  239.3 38.8 %copy-start = (f32[22,256,128]{2,1,0:T(8,128)S(1)}, f32[22,256,128]{2,1,0:T(8,128)}, u32[]{:S(2)}) copy-start(f32[22,256,128]{2,1,0:T(8,128)} %all-reduce.3.cloned.1.call-done) | copy-start | bytes 8650756
  240.9 37.2 %collective-permute-start.2 = (f32[22,128,128]{2,1,0:T(8,128)S(1)}, f32[22,128,128]{2,1,0:T(8,128)S(1)}, u32[]{:S(2)}, u32[]{:S(2)}) collective-permute-start(f32[22,128,128]{2,1,0:T(8,128)S(1)} %slice.766), channel_id=1, source_target_pairs={{0,16},{16,32},{32,48},{48,64},{64,80},{80,96},{96,112},{112,128},... | collective-permute-start | bytes 4325384 | tf_op jit(solution)/shard_map/ppermute | solution.py:21
  279.4 33.0 %collective-permute-start.3 = (f32[22,128,128]{2,1,0:T(8,128)S(1)}, f32[22,128,128]{2,1,0:T(8,128)S(1)}, u32[]{:S(2)}, u32[]{:S(2)}) collective-permute-start(f32[22,128,128]{2,1,0:T(8,128)S(1)} %bitcast_dynamic-update-slice_fusion), channel_id=1, source_target_pairs={{0,496},{16,0},{32,16},{48,32},{64,48},{80,64},{96,80},{112,96},{1... | collective-permute-start | bytes 4325384 | tf_op jit(solution)/shard_map/ppermute | solution.py:21
  330.8 28.8 %copy-start.6 = (f32[1,5,128]{2,1,0:T(8,128)S(1)}, f32[1,5,128]{2,1,0:T(8,128)}, u32[]{:S(2)}) copy-start(f32[1,5,128]{2,1,0:T(8,128)} %copy.379) | copy-start | bytes 7684 | tf_op jit(solution)/shard_map/while
  330.8 28.8 %copy-start.7 = (f32[1,5,128]{2,1,0:T(8,128)S(1)}, f32[1,5,128]{2,1,0:T(8,128)}, u32[]{:S(2)}) copy-start(f32[1,5,128]{2,1,0:T(8,128)} %copy.380) | copy-start | bytes 7684 | tf_op jit(solution)/shard_map/while
  330.9 28.8 %copy-start.8 = (f32[1,5,128]{2,1,0:T(8,128)S(1)}, f32[1,5,128]{2,1,0:T(8,128)}, u32[]{:S(2)}) copy-start(f32[1,5,128]{2,1,0:T(8,128)} %copy.381) | copy-start | bytes 7684 | tf_op jit(solution)/shard_map/while
  330.9 28.8 %copy-start.9 = (f32[1,5,128]{2,1,0:T(8,128)S(1)}, f32[1,5,128]{2,1,0:T(8,128)}, u32[]{:S(2)}) copy-start(f32[1,5,128]{2,1,0:T(8,128)} %copy.384) | copy-start | bytes 7684 | tf_op jit(solution)/shard_map/while
  330.9 28.8 %copy-start.10 = (f32[1,5,128]{2,1,0:T(8,128)S(1)}, f32[1,5,128]{2,1,0:T(8,128)}, u32[]{:S(2)}) copy-start(f32[1,5,128]{2,1,0:T(8,128)} %copy.385) | copy-start | bytes 7684 | tf_op jit(solution)/shard_map/while
  330.9 28.8 %copy-start.12 = (f32[1,5,128]{2,1,0:T(8,128)S(1)}, f32[1,5,128]{2,1,0:T(8,128)}, u32[]{:S(2)}) copy-start(f32[1,5,128]{2,1,0:T(8,128)} %copy.386) | copy-start | bytes 7684 | tf_op jit(solution)/shard_map/while
  344.7 33.2 %copy-start.11 = (f32[1,5,128]{2,1,0:T(8,128)S(1)}, f32[1,5,128]{2,1,0:T(8,128)}, u32[]{:S(2)}) copy-start(f32[1,5,128]{2,1,0:T(8,128)} %copy.385) | copy-start | bytes 7684 | tf_op jit(solution)/shard_map/while
  402.2 28.8 %copy-start.6 = (f32[1,5,128]{2,1,0:T(8,128)S(1)}, f32[1,5,128]{2,1,0:T(8,128)}, u32[]{:S(2)}) copy-start(f32[1,5,128]{2,1,0:T(8,128)} %copy.379) | copy-start | bytes 7684 | tf_op jit(solution)/shard_map/while
  402.2 28.8 %copy-start.7 = (f32[1,5,128]{2,1,0:T(8,128)S(1)}, f32[1,5,128]{2,1,0:T(8,128)}, u32[]{:S(2)}) copy-start(f32[1,5,128]{2,1,0:T(8,128)} %copy.380) | copy-start | bytes 7684 | tf_op jit(solution)/shard_map/while
  402.2 28.8 %copy-start.8 = (f32[1,5,128]{2,1,0:T(8,128)S(1)}, f32[1,5,128]{2,1,0:T(8,128)}, u32[]{:S(2)}) copy-start(f32[1,5,128]{2,1,0:T(8,128)} %copy.381) | copy-start | bytes 7684 | tf_op jit(solution)/shard_map/while
  402.2 28.8 %copy-start.9 = (f32[1,5,128]{2,1,0:T(8,128)S(1)}, f32[1,5,128]{2,1,0:T(8,128)}, u32[]{:S(2)}) copy-start(f32[1,5,128]{2,1,0:T(8,128)} %copy.384) | copy-start | bytes 7684 | tf_op jit(solution)/shard_map/while
  402.2 28.8 %copy-start.10 = (f32[1,5,128]{2,1,0:T(8,128)S(1)}, f32[1,5,128]{2,1,0:T(8,128)}, u32[]{:S(2)}) copy-start(f32[1,5,128]{2,1,0:T(8,128)} %copy.385) | copy-start | bytes 7684 | tf_op jit(solution)/shard_map/while
  402.2 28.8 %copy-start.12 = (f32[1,5,128]{2,1,0:T(8,128)S(1)}, f32[1,5,128]{2,1,0:T(8,128)}, u32[]{:S(2)}) copy-start(f32[1,5,128]{2,1,0:T(8,128)} %copy.386) | copy-start | bytes 7684 | tf_op jit(solution)/shard_map/while
  416.0 33.2 %copy-start.11 = (f32[1,5,128]{2,1,0:T(8,128)S(1)}, f32[1,5,128]{2,1,0:T(8,128)}, u32[]{:S(2)}) copy-start(f32[1,5,128]{2,1,0:T(8,128)} %copy.385) | copy-start | bytes 7684 | tf_op jit(solution)/shard_map/while
  473.5 28.8 %copy-start.6 = (f32[1,5,128]{2,1,0:T(8,128)S(1)}, f32[1,5,128]{2,1,0:T(8,128)}, u32[]{:S(2)}) copy-start(f32[1,5,128]{2,1,0:T(8,128)} %copy.379) | copy-start | bytes 7684 | tf_op jit(solution)/shard_map/while
  473.5 28.8 %copy-start.7 = (f32[1,5,128]{2,1,0:T(8,128)S(1)}, f32[1,5,128]{2,1,0:T(8,128)}, u32[]{:S(2)}) copy-start(f32[1,5,128]{2,1,0:T(8,128)} %copy.380) | copy-start | bytes 7684 | tf_op jit(solution)/shard_map/while
  473.5 28.8 %copy-start.8 = (f32[1,5,128]{2,1,0:T(8,128)S(1)}, f32[1,5,128]{2,1,0:T(8,128)}, u32[]{:S(2)}) copy-start(f32[1,5,128]{2,1,0:T(8,128)} %copy.381) | copy-start | bytes 7684 | tf_op jit(solution)/shard_map/while
  473.5 28.8 %copy-start.9 = (f32[1,5,128]{2,1,0:T(8,128)S(1)}, f32[1,5,128]{2,1,0:T(8,128)}, u32[]{:S(2)}) copy-start(f32[1,5,128]{2,1,0:T(8,128)} %copy.384) | copy-start | bytes 7684 | tf_op jit(solution)/shard_map/while
  473.5 28.8 %copy-start.10 = (f32[1,5,128]{2,1,0:T(8,128)S(1)}, f32[1,5,128]{2,1,0:T(8,128)}, u32[]{:S(2)}) copy-start(f32[1,5,128]{2,1,0:T(8,128)} %copy.385) | copy-start | bytes 7684 | tf_op jit(solution)/shard_map/while
  473.5 28.8 %copy-start.12 = (f32[1,5,128]{2,1,0:T(8,128)S(1)}, f32[1,5,128]{2,1,0:T(8,128)}, u32[]{:S(2)}) copy-start(f32[1,5,128]{2,1,0:T(8,128)} %copy.386) | copy-start | bytes 7684 | tf_op jit(solution)/shard_map/while
  487.3 33.2 %copy-start.11 = (f32[1,5,128]{2,1,0:T(8,128)S(1)}, f32[1,5,128]{2,1,0:T(8,128)}, u32[]{:S(2)}) copy-start(f32[1,5,128]{2,1,0:T(8,128)} %copy.385) | copy-start | bytes 7684 | tf_op jit(solution)/shard_map/while
  544.8 28.8 %copy-start.6 = (f32[1,5,128]{2,1,0:T(8,128)S(1)}, f32[1,5,128]{2,1,0:T(8,128)}, u32[]{:S(2)}) copy-start(f32[1,5,128]{2,1,0:T(8,128)} %copy.379) | copy-start | bytes 7684 | tf_op jit(solution)/shard_map/while
  544.8 28.8 %copy-start.7 = (f32[1,5,128]{2,1,0:T(8,128)S(1)}, f32[1,5,128]{2,1,0:T(8,128)}, u32[]{:S(2)}) copy-start(f32[1,5,128]{2,1,0:T(8,128)} %copy.380) | copy-start | bytes 7684 | tf_op jit(solution)/shard_map/while
  544.8 28.8 %copy-start.8 = (f32[1,5,128]{2,1,0:T(8,128)S(1)}, f32[1,5,128]{2,1,0:T(8,128)}, u32[]{:S(2)}) copy-start(f32[1,5,128]{2,1,0:T(8,128)} %copy.381) | copy-start | bytes 7684 | tf_op jit(solution)/shard_map/while
  544.8 28.8 %copy-start.9 = (f32[1,5,128]{2,1,0:T(8,128)S(1)}, f32[1,5,128]{2,1,0:T(8,128)}, u32[]{:S(2)}) copy-start(f32[1,5,128]{2,1,0:T(8,128)} %copy.384) | copy-start | bytes 7684 | tf_op jit(solution)/shard_map/while
  544.8 28.8 %copy-start.10 = (f32[1,5,128]{2,1,0:T(8,128)S(1)}, f32[1,5,128]{2,1,0:T(8,128)}, u32[]{:S(2)}) copy-start(f32[1,5,128]{2,1,0:T(8,128)} %copy.385) | copy-start | bytes 7684 | tf_op jit(solution)/shard_map/while
  544.9 28.8 %copy-start.12 = (f32[1,5,128]{2,1,0:T(8,128)S(1)}, f32[1,5,128]{2,1,0:T(8,128)}, u32[]{:S(2)}) copy-start(f32[1,5,128]{2,1,0:T(8,128)} %copy.386) | copy-start | bytes 7684 | tf_op jit(solution)/shard_map/while
  558.6 33.2 %copy-start.11 = (f32[1,5,128]{2,1,0:T(8,128)S(1)}, f32[1,5,128]{2,1,0:T(8,128)}, u32[]{:S(2)}) copy-start(f32[1,5,128]{2,1,0:T(8,128)} %copy.385) | copy-start | bytes 7684 | tf_op jit(solution)/shard_map/while
  616.1 28.8 %copy-start.6 = (f32[1,5,128]{2,1,0:T(8,128)S(1)}, f32[1,5,128]{2,1,0:T(8,128)}, u32[]{:S(2)}) copy-start(f32[1,5,128]{2,1,0:T(8,128)} %copy.379) | copy-start | bytes 7684 | tf_op jit(solution)/shard_map/while
  616.1 28.8 %copy-start.7 = (f32[1,5,128]{2,1,0:T(8,128)S(1)}, f32[1,5,128]{2,1,0:T(8,128)}, u32[]{:S(2)}) copy-start(f32[1,5,128]{2,1,0:T(8,128)} %copy.380) | copy-start | bytes 7684 | tf_op jit(solution)/shard_map/while
  616.1 28.8 %copy-start.8 = (f32[1,5,128]{2,1,0:T(8,128)S(1)}, f32[1,5,128]{2,1,0:T(8,128)}, u32[]{:S(2)}) copy-start(f32[1,5,128]{2,1,0:T(8,128)} %copy.381) | copy-start | bytes 7684 | tf_op jit(solution)/shard_map/while
  616.2 28.8 %copy-start.9 = (f32[1,5,128]{2,1,0:T(8,128)S(1)}, f32[1,5,128]{2,1,0:T(8,128)}, u32[]{:S(2)}) copy-start(f32[1,5,128]{2,1,0:T(8,128)} %copy.384) | copy-start | bytes 7684 | tf_op jit(solution)/shard_map/while
  616.2 28.8 %copy-start.10 = (f32[1,5,128]{2,1,0:T(8,128)S(1)}, f32[1,5,128]{2,1,0:T(8,128)}, u32[]{:S(2)}) copy-start(f32[1,5,128]{2,1,0:T(8,128)} %copy.385) | copy-start | bytes 7684 | tf_op jit(solution)/shard_map/while
  616.2 28.8 %copy-start.12 = (f32[1,5,128]{2,1,0:T(8,128)S(1)}, f32[1,5,128]{2,1,0:T(8,128)}, u32[]{:S(2)}) copy-start(f32[1,5,128]{2,1,0:T(8,128)} %copy.386) | copy-start | bytes 7684 | tf_op jit(solution)/shard_map/while
  630.0 33.2 %copy-start.11 = (f32[1,5,128]{2,1,0:T(8,128)S(1)}, f32[1,5,128]{2,1,0:T(8,128)}, u32[]{:S(2)}) copy-start(f32[1,5,128]{2,1,0:T(8,128)} %copy.385) | copy-start | bytes 7684 | tf_op jit(solution)/shard_map/while
  687.4 28.8 %copy-start.6 = (f32[1,5,128]{2,1,0:T(8,128)S(1)}, f32[1,5,128]{2,1,0:T(8,128)}, u32[]{:S(2)}) copy-start(f32[1,5,128]{2,1,0:T(8,128)} %copy.379) | copy-start | bytes 7684 | tf_op jit(solution)/shard_map/while
  687.5 28.8 %copy-start.7 = (f32[1,5,128]{2,1,0:T(8,128)S(1)}, f32[1,5,128]{2,1,0:T(8,128)}, u32[]{:S(2)}) copy-start(f32[1,5,128]{2,1,0:T(8,128)} %copy.380) | copy-start | bytes 7684 | tf_op jit(solution)/shard_map/while
  687.5 28.8 %copy-start.8 = (f32[1,5,128]{2,1,0:T(8,128)S(1)}, f32[1,5,128]{2,1,0:T(8,128)}, u32[]{:S(2)}) copy-start(f32[1,5,128]{2,1,0:T(8,128)} %copy.381) | copy-start | bytes 7684 | tf_op jit(solution)/shard_map/while
  687.5 28.8 %copy-start.9 = (f32[1,5,128]{2,1,0:T(8,128)S(1)}, f32[1,5,128]{2,1,0:T(8,128)}, u32[]{:S(2)}) copy-start(f32[1,5,128]{2,1,0:T(8,128)} %copy.384) | copy-start | bytes 7684 | tf_op jit(solution)/shard_map/while
  687.5 28.8 %copy-start.10 = (f32[1,5,128]{2,1,0:T(8,128)S(1)}, f32[1,5,128]{2,1,0:T(8,128)}, u32[]{:S(2)}) copy-start(f32[1,5,128]{2,1,0:T(8,128)} %copy.385) | copy-start | bytes 7684 | tf_op jit(solution)/shard_map/while
  687.5 28.8 %copy-start.12 = (f32[1,5,128]{2,1,0:T(8,128)S(1)}, f32[1,5,128]{2,1,0:T(8,128)}, u32[]{:S(2)}) copy-start(f32[1,5,128]{2,1,0:T(8,128)} %copy.386) | copy-start | bytes 7684 | tf_op jit(solution)/shard_map/while
  701.3 33.2 %copy-start.11 = (f32[1,5,128]{2,1,0:T(8,128)S(1)}, f32[1,5,128]{2,1,0:T(8,128)}, u32[]{:S(2)}) copy-start(f32[1,5,128]{2,1,0:T(8,128)} %copy.385) | copy-start | bytes 7684 | tf_op jit(solution)/shard_map/while
  758.8 28.8 %copy-start.6 = (f32[1,5,128]{2,1,0:T(8,128)S(1)}, f32[1,5,128]{2,1,0:T(8,128)}, u32[]{:S(2)}) copy-start(f32[1,5,128]{2,1,0:T(8,128)} %copy.379) | copy-start | bytes 7684 | tf_op jit(solution)/shard_map/while
  758.8 28.8 %copy-start.7 = (f32[1,5,128]{2,1,0:T(8,128)S(1)}, f32[1,5,128]{2,1,0:T(8,128)}, u32[]{:S(2)}) copy-start(f32[1,5,128]{2,1,0:T(8,128)} %copy.380) | copy-start | bytes 7684 | tf_op jit(solution)/shard_map/while
  758.8 28.8 %copy-start.8 = (f32[1,5,128]{2,1,0:T(8,128)S(1)}, f32[1,5,128]{2,1,0:T(8,128)}, u32[]{:S(2)}) copy-start(f32[1,5,128]{2,1,0:T(8,128)} %copy.381) | copy-start | bytes 7684 | tf_op jit(solution)/shard_map/while
  758.8 28.8 %copy-start.9 = (f32[1,5,128]{2,1,0:T(8,128)S(1)}, f32[1,5,128]{2,1,0:T(8,128)}, u32[]{:S(2)}) copy-start(f32[1,5,128]{2,1,0:T(8,128)} %copy.384) | copy-start | bytes 7684 | tf_op jit(solution)/shard_map/while
  758.8 28.8 %copy-start.10 = (f32[1,5,128]{2,1,0:T(8,128)S(1)}, f32[1,5,128]{2,1,0:T(8,128)}, u32[]{:S(2)}) copy-start(f32[1,5,128]{2,1,0:T(8,128)} %copy.385) | copy-start | bytes 7684 | tf_op jit(solution)/shard_map/while
  758.8 28.8 %copy-start.12 = (f32[1,5,128]{2,1,0:T(8,128)S(1)}, f32[1,5,128]{2,1,0:T(8,128)}, u32[]{:S(2)}) copy-start(f32[1,5,128]{2,1,0:T(8,128)} %copy.386) | copy-start | bytes 7684 | tf_op jit(solution)/shard_map/while
  772.6 33.2 %copy-start.11 = (f32[1,5,128]{2,1,0:T(8,128)S(1)}, f32[1,5,128]{2,1,0:T(8,128)}, u32[]{:S(2)}) copy-start(f32[1,5,128]{2,1,0:T(8,128)} %copy.385) | copy-start | bytes 7684 | tf_op jit(solution)/shard_map/while
  830.1 28.8 %copy-start.6 = (f32[1,5,128]{2,1,0:T(8,128)S(1)}, f32[1,5,128]{2,1,0:T(8,128)}, u32[]{:S(2)}) copy-start(f32[1,5,128]{2,1,0:T(8,128)} %copy.379) | copy-start | bytes 7684 | tf_op jit(solution)/shard_map/while
  830.1 28.8 %copy-start.7 = (f32[1,5,128]{2,1,0:T(8,128)S(1)}, f32[1,5,128]{2,1,0:T(8,128)}, u32[]{:S(2)}) copy-start(f32[1,5,128]{2,1,0:T(8,128)} %copy.380) | copy-start | bytes 7684 | tf_op jit(solution)/shard_map/while
  830.1 28.8 %copy-start.8 = (f32[1,5,128]{2,1,0:T(8,128)S(1)}, f32[1,5,128]{2,1,0:T(8,128)}, u32[]{:S(2)}) copy-start(f32[1,5,128]{2,1,0:T(8,128)} %copy.381) | copy-start | bytes 7684 | tf_op jit(solution)/shard_map/while
  830.1 28.8 %copy-start.9 = (f32[1,5,128]{2,1,0:T(8,128)S(1)}, f32[1,5,128]{2,1,0:T(8,128)}, u32[]{:S(2)}) copy-start(f32[1,5,128]{2,1,0:T(8,128)} %copy.384) | copy-start | bytes 7684 | tf_op jit(solution)/shard_map/while
  830.1 28.8 %copy-start.10 = (f32[1,5,128]{2,1,0:T(8,128)S(1)}, f32[1,5,128]{2,1,0:T(8,128)}, u32[]{:S(2)}) copy-start(f32[1,5,128]{2,1,0:T(8,128)} %copy.385) | copy-start | bytes 7684 | tf_op jit(solution)/shard_map/while
  830.1 28.8 %copy-start.12 = (f32[1,5,128]{2,1,0:T(8,128)S(1)}, f32[1,5,128]{2,1,0:T(8,128)}, u32[]{:S(2)}) copy-start(f32[1,5,128]{2,1,0:T(8,128)} %copy.386) | copy-start | bytes 7684 | tf_op jit(solution)/shard_map/while
  843.9 33.2 %copy-start.11 = (f32[1,5,128]{2,1,0:T(8,128)S(1)}, f32[1,5,128]{2,1,0:T(8,128)}, u32[]{:S(2)}) copy-start(f32[1,5,128]{2,1,0:T(8,128)} %copy.385) | copy-start | bytes 7684 | tf_op jit(solution)/shard_map/while
  1007.5 13.8 %collective-permute-start.4 = (f32[5,128,128]{2,1,0:T(8,128)S(1)}, f32[5,128,128]{2,1,0:T(8,128)S(1)}, u32[]{:S(2)}, u32[]{:S(2)}) collective-permute-start(f32[5,128,128]{2,1,0:T(8,128)S(1)} %slice.791), channel_id=1, source_target_pairs={{0,16},{16,32},{32,48},{48,64},{64,80},{80,96},{96,112},{112,128},... | collective-permute-start | bytes 983048 | tf_op jit(solution)/shard_map/ppermute | solution.py:21
  (284 other events, 5810.3 us)
Sparse Core Ops, SparseCore 0:
  112.9 126.3 all-reduce.2
  889.2 117.2 all-reduce.4
where the time goes:
time: 1030 us
  local copies, waits for them, and re-layouts  334 us (32%)
  waiting for transfers between devices  321 us (31%)
  other arithmetic  318 us (31%)
  starting transfers between devices  20.2 us (2%)
  between operations  14.4 us (1%)
  loops' own time  12.5 us (1%)
    reduce_sum x40, other arithmetic, flux_tile(): jnp.sum(pair_scale * face_flux, axis=1)  246 us
    psum x2, waiting for transfers between devices, settle(): partial_value = lax.psum(partial_value, 'sub')  244 us
    while x1648, local copies, waits for them, and re-layouts  234 us
    ppermute x5, waiting for transfers between devices, shifted(): lax.ppermute(shard, axis, [(i, (i + by) % peers) for i in range(peers)])  77.5 us
    reduce_sum x16, other arithmetic, moment_tile(): col_sums = jnp.stack([jnp.sum(summand, axis=1) for summand in summands])  29.6 us
  transfers between devices with their start and end apart: 7, of which 6 were waited for; matrix products, arithmetic and copies ran while one was open for 1% of the time, Pallas kernels for 0%

commit v1 on v0

--- a/solution.py
+++ b/solution.py
@@ -14,6 +14,15 @@
 AREA_FLOOR = 0.0001
 SYM_PAIRS = ((0, 0), (0, 1), (0, 2), (1, 1), (1, 2), (2, 2))
 UNIT_DIAG = (1.0, 0.0, 0.0, 1.0, 0.0, 1.0)
+
+
+def add_in_pairs(block, name):
+    size = lax.axis_size(name)
+    total, far = (block, 1)
+    while far < size:
+        total = total + lax.ppermute(total, name, [(i, i ^ far) for i in range(size)])
+        far = 2 * far
+    return total
 
 
 def shifted(shard, axis, by):
@@ -318,7 +327,7 @@
 
     def settle(partial_value):
         row_count = partial_value.shape[0]
-        partial_value = lax.psum(partial_value, "sub")
+        partial_value = add_in_pairs(partial_value, "sub")
         own_part = partial_value[:, :slab_leaves]
         next_part = partial_value[:, slab_leaves:]
         returned = shifted(next_part, "slab", 1)

time: 1030 us -> 1200 us (1.17)
  waiting for transfers between devices: 321 us -> 473 us
  starting transfers between devices: 20.2 us -> 51.6 us
  between operations: 14.4 us -> 1.08 us
    ppermute x0 -> x8, waiting for transfers between devices: none -> 395 us  [add_in_pairs(): lax.ppermute(total, name, [(i, i ^ far) for i in range(size)])]
    psum x2 -> x0, waiting for transfers between devices: 244 us -> none  [settle(): partial_value = lax.psum(partial_value, 'sub')]
    ppermute x0 -> x8, starting transfers between devices: none -> 33.2 us  [add_in_pairs(): lax.ppermute(total, name, [(i, i ^ far) for i in range(size)])]
    while x1648 -> x1632, local copies, waits for them, and re-layouts: 234 us -> 239 us
  transfers between devices with their start and end apart: 7 -> 13, of which waited for: 6 -> 12; matrix products, arithmetic and copies ran while one was open for 1% -> 1% of each run, Pallas kernels for 0% -> 0%
where the time goes in v1:
time: 1200 us
  waiting for transfers between devices  473 us (39%)
  local copies, waits for them, and re-layouts  337 us (28%)
  other arithmetic  315 us (26%)
  starting transfers between devices  51.6 us (4%)
  loops' own time  12.1 us (1%)
    ppermute x8, waiting for transfers between devices, add_in_pairs(): lax.ppermute(total, name, [(i, i ^ far) for i in range(size)])  395 us
    reduce_sum x40, other arithmetic, flux_tile(): jnp.sum(pair_scale * face_flux, axis=1)  244 us
    while x1632, local copies, waits for them, and re-layouts  239 us
    ppermute x5, waiting for transfers between devices, shifted(): lax.ppermute(shard, axis, [(i, (i + by) % peers) for i in range(peers)])  77.4 us
    ppermute x8, starting transfers between devices, add_in_pairs(): lax.ppermute(total, name, [(i, i ^ far) for i in range(size)])  33.2 us
    reduce_sum x16, other arithmetic, moment_tile(): col_sums = jnp.stack([jnp.sum(summand, axis=1) for summand in summands])  29.5 us
  transfers between devices with their start and end apart: 13, of which 12 were waited for; matrix products, arithmetic and copies ran while one was open for 1% of the time, Pallas kernels for 0%

profile of v1, /device:TPU:1, one launch (start us, length us, event | category | flops | bytes accessed | tf_op | source)
XLA Modules:
  0.0 1196.5 jit_solution(10769122998254877427)
XLA Ops:
  0.7 8.1 collective-permute-start.1
  21.4 3.2 collective-permute-done
  25.8 73.7 %while.30 = (s32[]{:T(128)}, f32[22,40,128]{2,1,0:T(8,128)S(1)}, f32[22,40,128]{2,1,0:T(8,128)S(1)}, s32[]{:T(128)}, s32[40]{0:T(128)}, /*index=5*/f32[8,256,128...) while((s32[]{:T(128)}, f32[22,40,128]{2,1,0:T(8,128)S(1)}, ...), condition=%wide.region_47.49_spmd.clone, body=%wide.region_2.48_spmd.clone.sunk | while | flops 9721420 | bytes 1241347 | solution.py:322
  30.4 2.9 fusion.246
  39.7 2.9 fusion.246
  48.9 2.9 fusion.246
  58.1 2.9 fusion.246
  67.3 2.9 fusion.246
  85.8 2.9 fusion.246
  105.7 5.2 collective-permute-done.2
  113.3 63.9 %collective-permute-done.3 = f32[22,256,128]{2,1,0:T(8,128)S(1)} collective-permute-done((f32[22,256,128]{2,1,0:T(8,128)S(1)}, f32[22,256,128]{2,1,0:T(8,128)S(1)}, u32[]{:S(2)}, u32[]{:S(2)}) %collective-permute-start.3) | collective-permute-done | bytes 2883616 | tf_op jit(solution)/shard_map/ppermute | solution.py:23
  177.6 5.8 collective-permute-start.4
  183.4 124.7 %collective-permute-done.4 = f32[22,256,128]{2,1,0:T(8,128)S(1)} collective-permute-done((f32[22,256,128]{2,1,0:T(8,128)S(1)}, f32[22,256,128]{2,1,0:T(8,128)S(1)}, u32[]{:S(2)}, u32[]{:S(2)}) %collective-permute-start.4) | collective-permute-done | bytes 2883616 | tf_op jit(solution)/shard_map/ppermute | solution.py:23
  308.5 9.1 collective-permute-start.5
  317.6 123.9 %collective-permute-done.5 = f32[22,256,128]{2,1,0:T(8,128)S(1)} collective-permute-done((f32[22,256,128]{2,1,0:T(8,128)S(1)}, f32[22,256,128]{2,1,0:T(8,128)S(1)}, u32[]{:S(2)}, u32[]{:S(2)}) %collective-permute-start.5) | collective-permute-done | bytes 2883616 | tf_op jit(solution)/shard_map/ppermute | solution.py:23
  442.1 3.4 collective-permute-start.6
  445.5 32.9 %collective-permute-done.6 = f32[22,128,128]{2,1,0:T(8,128)S(1)} collective-permute-done((f32[22,128,128]{2,1,0:T(8,128)S(1)}, f32[22,128,128]{2,1,0:T(8,128)S(1)}, u32[]{:S(2)}, u32[]{:S(2)}) %collective-permute-start.6) | collective-permute-done | bytes 1441824 | tf_op jit(solution)/shard_map/ppermute | solution.py:30
  482.1 29.6 %collective-permute-done.7 = f32[22,128,128]{2,1,0:T(8,128)S(1)} collective-permute-done((f32[22,128,128]{2,1,0:T(8,128)S(1)}, f32[22,128,128]{2,1,0:T(8,128)S(1)}, u32[]{:S(2)}, u32[]{:S(2)}) %collective-permute-start.7) | collective-permute-done | bytes 1441824 | tf_op jit(solution)/shard_map/ppermute | solution.py:30
  514.3 572.5 %while.31 = (s32[]{:T(128)}, f32[5,40,128]{2,1,0:T(8,128)}, f32[5,40,128]{2,1,0:T(8,128)S(1)}, s32[]{:T(128)}, s32[40]{0:T(128)}, /*index=5*/f32[8,256,128]{2,0,...) while((s32[]{:T(128)}, f32[5,40,128]{2,1,0:T(8,128)}, ...), condition=%wide.region_59.62_spmd.clone, body=%wide.region_48.61_spmd.clone.sunk | while | flops 113486544 | bytes 2750965 | solution.py:322
  553.3 6.3 fusion.254
  559.6 5.9 fusion.253
  565.6 6.2 fusion.255
  572.1 5.5 fusion.256
  577.6 6.7 fusion.257
  624.8 6.3 fusion.254
  631.2 5.9 fusion.253
  637.1 6.2 fusion.255
  643.7 5.5 fusion.256
  649.2 6.7 fusion.257
  696.4 6.3 fusion.254
  702.8 5.9 fusion.253
  708.7 6.2 fusion.255
  715.2 5.5 fusion.256
  720.7 6.7 fusion.257
  767.9 6.3 fusion.254
  774.3 5.9 fusion.253
  780.2 6.2 fusion.255
  786.8 5.5 fusion.256
  792.3 6.7 fusion.257
  839.5 6.3 fusion.254
  845.9 5.9 fusion.253
  851.8 6.2 fusion.255
  858.3 5.5 fusion.256
  863.8 6.7 fusion.257
  911.1 6.3 fusion.254
  917.4 5.9 fusion.253
  923.4 6.2 fusion.255
  929.9 5.5 fusion.256
  935.4 6.7 fusion.257
  982.6 6.3 fusion.254
  989.0 5.9 fusion.253
  994.9 6.2 fusion.255
  1001.5 5.5 fusion.256
  1007.0 6.7 fusion.257
  1054.2 6.3 fusion.254
  1060.6 5.9 fusion.253
  1066.5 6.2 fusion.255
  1073.0 5.5 fusion.256
  1078.5 6.7 fusion.257
  1095.4 16.1 %collective-permute-done.9 = f32[5,256,128]{2,1,0:T(8,128)S(1)} collective-permute-done((f32[5,256,128]{2,1,0:T(8,128)S(1)}, f32[5,256,128]{2,1,0:T(8,128)S(1)}, u32[]{:S(2)}, u32[]{:S(2)}) %collective-permute-start.9) | collective-permute-done | bytes 655392 | tf_op jit(solution)/shard_map/ppermute | solution.py:23
  1113.6 31.6 %collective-permute-done.10 = f32[5,256,128]{2,1,0:T(8,128)S(1)} collective-permute-done((f32[5,256,128]{2,1,0:T(8,128)S(1)}, f32[5,256,128]{2,1,0:T(8,128)S(1)}, u32[]{:S(2)}, u32[]{:S(2)}) %collective-permute-start.10) | collective-permute-done | bytes 655392 | tf_op jit(solution)/shard_map/ppermute | solution.py:23
  1145.2 8.7 collective-permute-start.11
  1153.9 27.9 %collective-permute-done.11 = f32[5,256,128]{2,1,0:T(8,128)S(1)} collective-permute-done((f32[5,256,128]{2,1,0:T(8,128)S(1)}, f32[5,256,128]{2,1,0:T(8,128)S(1)}, u32[]{:S(2)}, u32[]{:S(2)}) %collective-permute-start.11) | collective-permute-done | bytes 655392 | tf_op jit(solution)/shard_map/ppermute | solution.py:23
  1183.8 11.6 collective-permute-done.12
  (2204 shorter events, 415.9 us)
Async XLA Ops:
  0.7 20.0 %collective-permute-start.1 = (f32[128]{0:T(128)S(1)}, f32[128]{0:T(128)S(1)}, u32[]{:S(2)}, u32[]{:S(2)}) collective-permute-start(f32[128]{0:T(128)S(1)} %convert_element_type.36), channel_id=1, source_target_pairs={{0,496},{16,0},{32,16},{48,32},{64,48},{80,64},{96,80},{112,96},{1... | collective-permute-start | bytes 1544 | tf_op jit(solution)/shard_map/ppermute | solution.py:30
  10.2 14.4 %collective-permute-start = (f32[8,16384]{1,0:T(8,128)S(1)}, f32[8,16384]{1,0:T(8,128)S(1)}, u32[]{:S(2)}, u32[]{:S(2)}) collective-permute-start(f32[8,16384]{1,0:T(8,128)S(1)} %pad_maximum_fusion.2), channel_id=1, source_target_pairs={{0,496},{16,0},{32,16},{48,32},{64,48},{80,64},{96,80},{112,96},{1... | collective-permute-start | bytes 1572872 | tf_op jit(solution)/shard_map/ppermute | solution.py:30
  103.8 7.2 collective-permute-start.2
  111.4 65.8 %collective-permute-start.3 = (f32[22,256,128]{2,1,0:T(8,128)S(1)}, f32[22,256,128]{2,1,0:T(8,128)S(1)}, u32[]{:S(2)}, u32[]{:S(2)}) collective-permute-start(f32[22,256,128]{2,1,0:T(8,128)S(1)} %add.914), channel_id=1, source_target_pairs={{0,2},{1,3},{2,0},{3,1},{4,6},{5,7},{6,4},{7,5},{8,10},{9,11},{10,... | collective-permute-start | bytes 8650760 | tf_op jit(solution)/shard_map/ppermute | solution.py:23
  177.6 130.5 %collective-permute-start.4 = (f32[22,256,128]{2,1,0:T(8,128)S(1)}, f32[22,256,128]{2,1,0:T(8,128)S(1)}, u32[]{:S(2)}, u32[]{:S(2)}) collective-permute-start(f32[22,256,128]{2,1,0:T(8,128)S(1)} %add.915), channel_id=1, source_target_pairs={{0,4},{1,5},{2,6},{3,7},{4,0},{5,1},{6,2},{7,3},{8,12},{9,13},{10,... | collective-permute-start | bytes 8650760 | tf_op jit(solution)/shard_map/ppermute | solution.py:23
  308.5 133.1 %collective-permute-start.5 = (f32[22,256,128]{2,1,0:T(8,128)S(1)}, f32[22,256,128]{2,1,0:T(8,128)S(1)}, u32[]{:S(2)}, u32[]{:S(2)}) collective-permute-start(f32[22,256,128]{2,1,0:T(8,128)S(1)} %add.916), channel_id=1, source_target_pairs={{0,8},{1,9},{2,10},{3,11},{4,12},{5,13},{6,14},{7,15},{8,0},{9,1},... | collective-permute-start | bytes 8650760 | tf_op jit(solution)/shard_map/ppermute | solution.py:23
  442.1 36.3 %collective-permute-start.6 = (f32[22,128,128]{2,1,0:T(8,128)S(1)}, f32[22,128,128]{2,1,0:T(8,128)S(1)}, u32[]{:S(2)}, u32[]{:S(2)}) collective-permute-start(f32[22,128,128]{2,1,0:T(8,128)S(1)} %slice.766), channel_id=1, source_target_pairs={{0,16},{16,32},{32,48},{48,64},{64,80},{80,96},{96,112},{112,128},... | collective-permute-start | bytes 4325384 | tf_op jit(solution)/shard_map/ppermute | solution.py:30
  479.6 32.1 %collective-permute-start.7 = (f32[22,128,128]{2,1,0:T(8,128)S(1)}, f32[22,128,128]{2,1,0:T(8,128)S(1)}, u32[]{:S(2)}, u32[]{:S(2)}) collective-permute-start(f32[22,128,128]{2,1,0:T(8,128)S(1)} %bitcast_dynamic-update-slice_fusion), channel_id=1, source_target_pairs={{0,496},{16,0},{32,16},{48,32},{64,48},{80,64},{96,80},{112,96},{1... | collective-permute-start | bytes 4325384 | tf_op jit(solution)/shard_map/ppermute | solution.py:30
  530.1 29.5 %copy-start.5 = (f32[1,5,128]{2,1,0:T(8,128)S(1)}, f32[1,5,128]{2,1,0:T(8,128)}, u32[]{:S(2)}) copy-start(f32[1,5,128]{2,1,0:T(8,128)} %copy.379) | copy-start | bytes 7684 | tf_op jit(solution)/shard_map/while
  530.1 29.5 %copy-start.6 = (f32[1,5,128]{2,1,0:T(8,128)S(1)}, f32[1,5,128]{2,1,0:T(8,128)}, u32[]{:S(2)}) copy-start(f32[1,5,128]{2,1,0:T(8,128)} %copy.380) | copy-start | bytes 7684 | tf_op jit(solution)/shard_map/while
  530.1 29.5 %copy-start.7 = (f32[1,5,128]{2,1,0:T(8,128)S(1)}, f32[1,5,128]{2,1,0:T(8,128)}, u32[]{:S(2)}) copy-start(f32[1,5,128]{2,1,0:T(8,128)} %copy.381) | copy-start | bytes 7684 | tf_op jit(solution)/shard_map/while
  530.1 29.5 %copy-start.8 = (f32[1,5,128]{2,1,0:T(8,128)S(1)}, f32[1,5,128]{2,1,0:T(8,128)}, u32[]{:S(2)}) copy-start(f32[1,5,128]{2,1,0:T(8,128)} %copy.384) | copy-start | bytes 7684 | tf_op jit(solution)/shard_map/while
  530.1 29.5 %copy-start.9 = (f32[1,5,128]{2,1,0:T(8,128)S(1)}, f32[1,5,128]{2,1,0:T(8,128)}, u32[]{:S(2)}) copy-start(f32[1,5,128]{2,1,0:T(8,128)} %copy.385) | copy-start | bytes 7684 | tf_op jit(solution)/shard_map/while
  530.2 29.5 %copy-start.10 = (f32[1,5,128]{2,1,0:T(8,128)S(1)}, f32[1,5,128]{2,1,0:T(8,128)}, u32[]{:S(2)}) copy-start(f32[1,5,128]{2,1,0:T(8,128)} %copy.386) | copy-start | bytes 7684 | tf_op jit(solution)/shard_map/while
  530.2 29.5 %copy-start.11 = (f32[1,5,128]{2,1,0:T(8,128)S(1)}, f32[1,5,128]{2,1,0:T(8,128)}, u32[]{:S(2)}) copy-start(f32[1,5,128]{2,1,0:T(8,128)} %copy.389) | copy-start | bytes 7684 | tf_op jit(solution)/shard_map/while
  530.2 29.5 %copy-start.12 = (f32[1,5,128]{2,1,0:T(8,128)S(1)}, f32[1,5,128]{2,1,0:T(8,128)}, u32[]{:S(2)}) copy-start(f32[1,5,128]{2,1,0:T(8,128)} %copy.390) | copy-start | bytes 7684 | tf_op jit(solution)/shard_map/while
  601.7 29.5 %copy-start.5 = (f32[1,5,128]{2,1,0:T(8,128)S(1)}, f32[1,5,128]{2,1,0:T(8,128)}, u32[]{:S(2)}) copy-start(f32[1,5,128]{2,1,0:T(8,128)} %copy.379) | copy-start | bytes 7684 | tf_op jit(solution)/shard_map/while
  601.7 29.5 %copy-start.6 = (f32[1,5,128]{2,1,0:T(8,128)S(1)}, f32[1,5,128]{2,1,0:T(8,128)}, u32[]{:S(2)}) copy-start(f32[1,5,128]{2,1,0:T(8,128)} %copy.380) | copy-start | bytes 7684 | tf_op jit(solution)/shard_map/while
  601.7 29.5 %copy-start.7 = (f32[1,5,128]{2,1,0:T(8,128)S(1)}, f32[1,5,128]{2,1,0:T(8,128)}, u32[]{:S(2)}) copy-start(f32[1,5,128]{2,1,0:T(8,128)} %copy.381) | copy-start | bytes 7684 | tf_op jit(solution)/shard_map/while
  601.7 29.5 %copy-start.8 = (f32[1,5,128]{2,1,0:T(8,128)S(1)}, f32[1,5,128]{2,1,0:T(8,128)}, u32[]{:S(2)}) copy-start(f32[1,5,128]{2,1,0:T(8,128)} %copy.384) | copy-start | bytes 7684 | tf_op jit(solution)/shard_map/while
  601.7 29.5 %copy-start.9 = (f32[1,5,128]{2,1,0:T(8,128)S(1)}, f32[1,5,128]{2,1,0:T(8,128)}, u32[]{:S(2)}) copy-start(f32[1,5,128]{2,1,0:T(8,128)} %copy.385) | copy-start | bytes 7684 | tf_op jit(solution)/shard_map/while
  601.7 29.5 %copy-start.10 = (f32[1,5,128]{2,1,0:T(8,128)S(1)}, f32[1,5,128]{2,1,0:T(8,128)}, u32[]{:S(2)}) copy-start(f32[1,5,128]{2,1,0:T(8,128)} %copy.386) | copy-start | bytes 7684 | tf_op jit(solution)/shard_map/while
  601.7 29.5 %copy-start.11 = (f32[1,5,128]{2,1,0:T(8,128)S(1)}, f32[1,5,128]{2,1,0:T(8,128)}, u32[]{:S(2)}) copy-start(f32[1,5,128]{2,1,0:T(8,128)} %copy.389) | copy-start | bytes 7684 | tf_op jit(solution)/shard_map/while
  601.7 29.5 %copy-start.12 = (f32[1,5,128]{2,1,0:T(8,128)S(1)}, f32[1,5,128]{2,1,0:T(8,128)}, u32[]{:S(2)}) copy-start(f32[1,5,128]{2,1,0:T(8,128)} %copy.390) | copy-start | bytes 7684 | tf_op jit(solution)/shard_map/while
  673.2 29.5 %copy-start.5 = (f32[1,5,128]{2,1,0:T(8,128)S(1)}, f32[1,5,128]{2,1,0:T(8,128)}, u32[]{:S(2)}) copy-start(f32[1,5,128]{2,1,0:T(8,128)} %copy.379) | copy-start | bytes 7684 | tf_op jit(solution)/shard_map/while
  673.2 29.5 %copy-start.6 = (f32[1,5,128]{2,1,0:T(8,128)S(1)}, f32[1,5,128]{2,1,0:T(8,128)}, u32[]{:S(2)}) copy-start(f32[1,5,128]{2,1,0:T(8,128)} %copy.380) | copy-start | bytes 7684 | tf_op jit(solution)/shard_map/while
  673.2 29.5 %copy-start.7 = (f32[1,5,128]{2,1,0:T(8,128)S(1)}, f32[1,5,128]{2,1,0:T(8,128)}, u32[]{:S(2)}) copy-start(f32[1,5,128]{2,1,0:T(8,128)} %copy.381) | copy-start | bytes 7684 | tf_op jit(solution)/shard_map/while
  673.3 29.5 %copy-start.8 = (f32[1,5,128]{2,1,0:T(8,128)S(1)}, f32[1,5,128]{2,1,0:T(8,128)}, u32[]{:S(2)}) copy-start(f32[1,5,128]{2,1,0:T(8,128)} %copy.384) | copy-start | bytes 7684 | tf_op jit(solution)/shard_map/while
  673.3 29.5 %copy-start.9 = (f32[1,5,128]{2,1,0:T(8,128)S(1)}, f32[1,5,128]{2,1,0:T(8,128)}, u32[]{:S(2)}) copy-start(f32[1,5,128]{2,1,0:T(8,128)} %copy.385) | copy-start | bytes 7684 | tf_op jit(solution)/shard_map/while
  673.3 29.5 %copy-start.10 = (f32[1,5,128]{2,1,0:T(8,128)S(1)}, f32[1,5,128]{2,1,0:T(8,128)}, u32[]{:S(2)}) copy-start(f32[1,5,128]{2,1,0:T(8,128)} %copy.386) | copy-start | bytes 7684 | tf_op jit(solution)/shard_map/while
  673.3 29.5 %copy-start.11 = (f32[1,5,128]{2,1,0:T(8,128)S(1)}, f32[1,5,128]{2,1,0:T(8,128)}, u32[]{:S(2)}) copy-start(f32[1,5,128]{2,1,0:T(8,128)} %copy.389) | copy-start | bytes 7684 | tf_op jit(solution)/shard_map/while
  673.3 29.5 %copy-start.12 = (f32[1,5,128]{2,1,0:T(8,128)S(1)}, f32[1,5,128]{2,1,0:T(8,128)}, u32[]{:S(2)}) copy-start(f32[1,5,128]{2,1,0:T(8,128)} %copy.390) | copy-start | bytes 7684 | tf_op jit(solution)/shard_map/while
  744.8 29.5 %copy-start.5 = (f32[1,5,128]{2,1,0:T(8,128)S(1)}, f32[1,5,128]{2,1,0:T(8,128)}, u32[]{:S(2)}) copy-start(f32[1,5,128]{2,1,0:T(8,128)} %copy.379) | copy-start | bytes 7684 | tf_op jit(solution)/shard_map/while
  744.8 29.5 %copy-start.6 = (f32[1,5,128]{2,1,0:T(8,128)S(1)}, f32[1,5,128]{2,1,0:T(8,128)}, u32[]{:S(2)}) copy-start(f32[1,5,128]{2,1,0:T(8,128)} %copy.380) | copy-start | bytes 7684 | tf_op jit(solution)/shard_map/while
  744.8 29.5 %copy-start.7 = (f32[1,5,128]{2,1,0:T(8,128)S(1)}, f32[1,5,128]{2,1,0:T(8,128)}, u32[]{:S(2)}) copy-start(f32[1,5,128]{2,1,0:T(8,128)} %copy.381) | copy-start | bytes 7684 | tf_op jit(solution)/shard_map/while
  744.8 29.5 %copy-start.8 = (f32[1,5,128]{2,1,0:T(8,128)S(1)}, f32[1,5,128]{2,1,0:T(8,128)}, u32[]{:S(2)}) copy-start(f32[1,5,128]{2,1,0:T(8,128)} %copy.384) | copy-start | bytes 7684 | tf_op jit(solution)/shard_map/while
  744.8 29.5 %copy-start.9 = (f32[1,5,128]{2,1,0:T(8,128)S(1)}, f32[1,5,128]{2,1,0:T(8,128)}, u32[]{:S(2)}) copy-start(f32[1,5,128]{2,1,0:T(8,128)} %copy.385) | copy-start | bytes 7684 | tf_op jit(solution)/shard_map/while
  744.8 29.5 %copy-start.10 = (f32[1,5,128]{2,1,0:T(8,128)S(1)}, f32[1,5,128]{2,1,0:T(8,128)}, u32[]{:S(2)}) copy-start(f32[1,5,128]{2,1,0:T(8,128)} %copy.386) | copy-start | bytes 7684 | tf_op jit(solution)/shard_map/while
  744.8 29.5 %copy-start.11 = (f32[1,5,128]{2,1,0:T(8,128)S(1)}, f32[1,5,128]{2,1,0:T(8,128)}, u32[]{:S(2)}) copy-start(f32[1,5,128]{2,1,0:T(8,128)} %copy.389) | copy-start | bytes 7684 | tf_op jit(solution)/shard_map/while
  744.9 29.5 %copy-start.12 = (f32[1,5,128]{2,1,0:T(8,128)S(1)}, f32[1,5,128]{2,1,0:T(8,128)}, u32[]{:S(2)}) copy-start(f32[1,5,128]{2,1,0:T(8,128)} %copy.390) | copy-start | bytes 7684 | tf_op jit(solution)/shard_map/while
  816.3 29.5 %copy-start.5 = (f32[1,5,128]{2,1,0:T(8,128)S(1)}, f32[1,5,128]{2,1,0:T(8,128)}, u32[]{:S(2)}) copy-start(f32[1,5,128]{2,1,0:T(8,128)} %copy.379) | copy-start | bytes 7684 | tf_op jit(solution)/shard_map/while
  816.4 29.5 %copy-start.6 = (f32[1,5,128]{2,1,0:T(8,128)S(1)}, f32[1,5,128]{2,1,0:T(8,128)}, u32[]{:S(2)}) copy-start(f32[1,5,128]{2,1,0:T(8,128)} %copy.380) | copy-start | bytes 7684 | tf_op jit(solution)/shard_map/while
  816.4 29.5 %copy-start.7 = (f32[1,5,128]{2,1,0:T(8,128)S(1)}, f32[1,5,128]{2,1,0:T(8,128)}, u32[]{:S(2)}) copy-start(f32[1,5,128]{2,1,0:T(8,128)} %copy.381) | copy-start | bytes 7684 | tf_op jit(solution)/shard_map/while
  887.9 29.5 %copy-start.5 = (f32[1,5,128]{2,1,0:T(8,128)S(1)}, f32[1,5,128]{2,1,0:T(8,128)}, u32[]{:S(2)}) copy-start(f32[1,5,128]{2,1,0:T(8,128)} %copy.379) | copy-start | bytes 7684 | tf_op jit(solution)/shard_map/while
  887.9 29.5 %copy-start.6 = (f32[1,5,128]{2,1,0:T(8,128)S(1)}, f32[1,5,128]{2,1,0:T(8,128)}, u32[]{:S(2)}) copy-start(f32[1,5,128]{2,1,0:T(8,128)} %copy.380) | copy-start | bytes 7684 | tf_op jit(solution)/shard_map/while
  887.9 29.5 %copy-start.7 = (f32[1,5,128]{2,1,0:T(8,128)S(1)}, f32[1,5,128]{2,1,0:T(8,128)}, u32[]{:S(2)}) copy-start(f32[1,5,128]{2,1,0:T(8,128)} %copy.381) | copy-start | bytes 7684 | tf_op jit(solution)/shard_map/while
  887.9 29.5 %copy-start.8 = (f32[1,5,128]{2,1,0:T(8,128)S(1)}, f32[1,5,128]{2,1,0:T(8,128)}, u32[]{:S(2)}) copy-start(f32[1,5,128]{2,1,0:T(8,128)} %copy.384) | copy-start | bytes 7684 | tf_op jit(solution)/shard_map/while
  887.9 29.5 %copy-start.9 = (f32[1,5,128]{2,1,0:T(8,128)S(1)}, f32[1,5,128]{2,1,0:T(8,128)}, u32[]{:S(2)}) copy-start(f32[1,5,128]{2,1,0:T(8,128)} %copy.385) | copy-start | bytes 7684 | tf_op jit(solution)/shard_map/while
  888.0 29.5 %copy-start.10 = (f32[1,5,128]{2,1,0:T(8,128)S(1)}, f32[1,5,128]{2,1,0:T(8,128)}, u32[]{:S(2)}) copy-start(f32[1,5,128]{2,1,0:T(8,128)} %copy.386) | copy-start | bytes 7684 | tf_op jit(solution)/shard_map/while
  888.0 29.5 %copy-start.11 = (f32[1,5,128]{2,1,0:T(8,128)S(1)}, f32[1,5,128]{2,1,0:T(8,128)}, u32[]{:S(2)}) copy-start(f32[1,5,128]{2,1,0:T(8,128)} %copy.389) | copy-start | bytes 7684 | tf_op jit(solution)/shard_map/while
  888.0 29.5 %copy-start.12 = (f32[1,5,128]{2,1,0:T(8,128)S(1)}, f32[1,5,128]{2,1,0:T(8,128)}, u32[]{:S(2)}) copy-start(f32[1,5,128]{2,1,0:T(8,128)} %copy.390) | copy-start | bytes 7684 | tf_op jit(solution)/shard_map/while
  959.5 29.5 %copy-start.5 = (f32[1,5,128]{2,1,0:T(8,128)S(1)}, f32[1,5,128]{2,1,0:T(8,128)}, u32[]{:S(2)}) copy-start(f32[1,5,128]{2,1,0:T(8,128)} %copy.379) | copy-start | bytes 7684 | tf_op jit(solution)/shard_map/while
  959.5 29.5 %copy-start.6 = (f32[1,5,128]{2,1,0:T(8,128)S(1)}, f32[1,5,128]{2,1,0:T(8,128)}, u32[]{:S(2)}) copy-start(f32[1,5,128]{2,1,0:T(8,128)} %copy.380) | copy-start | bytes 7684 | tf_op jit(solution)/shard_map/while
  959.5 29.5 %copy-start.7 = (f32[1,5,128]{2,1,0:T(8,128)S(1)}, f32[1,5,128]{2,1,0:T(8,128)}, u32[]{:S(2)}) copy-start(f32[1,5,128]{2,1,0:T(8,128)} %copy.381) | copy-start | bytes 7684 | tf_op jit(solution)/shard_map/while
  959.5 29.5 %copy-start.8 = (f32[1,5,128]{2,1,0:T(8,128)S(1)}, f32[1,5,128]{2,1,0:T(8,128)}, u32[]{:S(2)}) copy-start(f32[1,5,128]{2,1,0:T(8,128)} %copy.384) | copy-start | bytes 7684 | tf_op jit(solution)/shard_map/while
  959.5 29.5 %copy-start.9 = (f32[1,5,128]{2,1,0:T(8,128)S(1)}, f32[1,5,128]{2,1,0:T(8,128)}, u32[]{:S(2)}) copy-start(f32[1,5,128]{2,1,0:T(8,128)} %copy.385) | copy-start | bytes 7684 | tf_op jit(solution)/shard_map/while
  959.5 29.5 %copy-start.10 = (f32[1,5,128]{2,1,0:T(8,128)S(1)}, f32[1,5,128]{2,1,0:T(8,128)}, u32[]{:S(2)}) copy-start(f32[1,5,128]{2,1,0:T(8,128)} %copy.386) | copy-start | bytes 7684 | tf_op jit(solution)/shard_map/while
  959.5 29.5 %copy-start.11 = (f32[1,5,128]{2,1,0:T(8,128)S(1)}, f32[1,5,128]{2,1,0:T(8,128)}, u32[]{:S(2)}) copy-start(f32[1,5,128]{2,1,0:T(8,128)} %copy.389) | copy-start | bytes 7684 | tf_op jit(solution)/shard_map/while
  959.5 29.5 %copy-start.12 = (f32[1,5,128]{2,1,0:T(8,128)S(1)}, f32[1,5,128]{2,1,0:T(8,128)}, u32[]{:S(2)}) copy-start(f32[1,5,128]{2,1,0:T(8,128)} %copy.390) | copy-start | bytes 7684 | tf_op jit(solution)/shard_map/while
  1089.4 4.0 collective-permute-start.8
  1093.5 18.0 %collective-permute-start.9 = (f32[5,256,128]{2,1,0:T(8,128)S(1)}, f32[5,256,128]{2,1,0:T(8,128)S(1)}, u32[]{:S(2)}, u32[]{:S(2)}) collective-permute-start(f32[5,256,128]{2,1,0:T(8,128)S(1)} %add.958), channel_id=1, source_target_pairs={{0,2},{1,3},{2,0},{3,1},{4,6},{5,7},{6,4},{7,5},{8,10},{9,11},{10,... | collective-permute-start | bytes 1966088 | tf_op jit(solution)/shard_map/ppermute | solution.py:23
  1111.6 33.5 %collective-permute-start.10 = (f32[5,256,128]{2,1,0:T(8,128)S(1)}, f32[5,256,128]{2,1,0:T(8,128)S(1)}, u32[]{:S(2)}, u32[]{:S(2)}) collective-permute-start(f32[5,256,128]{2,1,0:T(8,128)S(1)} %add.959), channel_id=1, source_target_pairs={{0,4},{1,5},{2,6},{3,7},{4,0},{5,1},{6,2},{7,3},{8,12},{9,13},{10,... | collective-permute-start | bytes 1966088 | tf_op jit(solution)/shard_map/ppermute | solution.py:23
  1145.2 36.6 %collective-permute-start.11 = (f32[5,256,128]{2,1,0:T(8,128)S(1)}, f32[5,256,128]{2,1,0:T(8,128)S(1)}, u32[]{:S(2)}, u32[]{:S(2)}) collective-permute-start(f32[5,256,128]{2,1,0:T(8,128)S(1)} %add.960), channel_id=1, source_target_pairs={{0,8},{1,9},{2,10},{3,11},{4,12},{5,13},{6,14},{7,15},{8,0},{9,1},... | collective-permute-start | bytes 1966088 | tf_op jit(solution)/shard_map/ppermute | solution.py:23
  1181.9 13.5 %collective-permute-start.12 = (f32[5,128,128]{2,1,0:T(8,128)S(1)}, f32[5,128,128]{2,1,0:T(8,128)S(1)}, u32[]{:S(2)}, u32[]{:S(2)}) collective-permute-start(f32[5,128,128]{2,1,0:T(8,128)S(1)} %slice.791), channel_id=1, source_target_pairs={{0,16},{16,32},{32,48},{48,64},{64,80},{80,96},{96,112},{112,128},... | collective-permute-start | bytes 983048 | tf_op jit(solution)/shard_map/ppermute | solution.py:30
  (281 other events, 5695.7 us)
